TPU v7x, 32 devices: a whole 2x2x4 slice. The times are simulated.
32 devices in a mesh: grp: 4 (over y, core), tm: 8 (over z, x).
Axes of the slice: x: 2, y: 2, z: 4, core: 2. Of those that a mesh axis runs over, the one named last changes fastest.
Arguments:
- wave: bfloat16 [4, 327680], P('grp', 'tm'), may hold values from -6 to 6
- assign: int32 [4, 1024], P('grp', 'tm'), may hold values from 0 to 16383
- w_first: bfloat16 [10, 512], replicated, may hold values from -2 to 2
- w_mid: bfloat16 [4, 1536, 512], replicated, may hold values from -0.15625 to 0.15625
- w_tail: bfloat16 [2, 1024, 512], replicated, may hold values from -0.1875 to 0.1875
- w_proj: bfloat16 [512, 768], replicated, may hold values from -0.25 to 0.25
- centroids: float32 [16384, 768], P('tm'), may hold values from -6 to 6
- prior: float32 [16384], P('tm'), may hold values from 1 to 16
Outputs:
- new_centroids: float32 [16384, 768], P('tm')
- new_counts: float32 [16384], P('tm')
- distortion: float32 [4, 1024], P('grp', 'tm')
All inputs are finite; a program needn't handle non-finite values.
Results may differ from a plain program's by a relative error of at most 0.007.
Values may be sent and summed in bfloat16 or wider, within the bound.
A program may use at most 128 MiB of HBM per device.

v0:
```python
import jax
import jax.numpy as jnp
from jax import lax
from jax.sharding import PartitionSpec as P

HALO = 80
EPS = 1e-05


def passed_along(value, axis, steps):
    count = lax.axis_size(axis)
    leading, last = (max(0, -steps), min(count, count - steps))
    return lax.ppermute(value, axis, [(source, source + steps) for source in range(leading, last)])


def norm_rows(accum):
    row_mean = jnp.mean(accum, axis=-1, keepdims=True)
    centred = accum - row_mean
    spread = jnp.mean(centred * centred, axis=-1, keepdims=True)
    return centred * lax.rsqrt(spread + EPS)


def activate(accum):
    return jax.nn.gelu(norm_rows(accum), approximate=False).astype(jnp.bfloat16)


def first_layer(samples, w_first):
    windows = samples.reshape(-1, 5)
    accum = jnp.dot(windows[:-1], w_first[:5], preferred_element_type=jnp.float32)
    accum = accum + jnp.dot(windows[1:], w_first[5:], preferred_element_type=jnp.float32)
    return activate(accum)


def odd_layer(inputs, weight):
    channels = inputs.shape[1]
    out_len = (inputs.shape[0] - 3) // 2 + 1
    paired = jnp.concatenate([inputs, jnp.zeros((1, channels), inputs.dtype)], axis=0).reshape(
        out_len + 1, 2 * channels
    )
    accum = jnp.dot(paired[:out_len], weight[: 2 * channels], preferred_element_type=jnp.float32)
    accum = accum + jnp.dot(
        paired[1:, :channels], weight[2 * channels :], preferred_element_type=jnp.float32
    )
    return activate(accum)


def even_layer(inputs, weight):
    channels = inputs.shape[1]
    paired = inputs.reshape(inputs.shape[0] // 2, 2 * channels)
    return activate(jnp.dot(paired, weight, preferred_element_type=jnp.float32))


def encode(samples, w_first, w_mid, w_tail):
    hidden = first_layer(samples, w_first)
    for layer_num in range(4):
        hidden = odd_layer(hidden, w_mid[layer_num])
    for layer_num in range(2):
        hidden = even_layer(hidden, w_tail[layer_num])
    return hidden


def project(features, w_proj):
    normed = norm_rows(features.astype(jnp.float32)).astype(jnp.bfloat16)
    return jnp.dot(normed, w_proj, preferred_element_type=jnp.float32).astype(jnp.bfloat16)


def local(wave, assign, w_first, w_mid, w_tail, w_proj, centroids, prior):
    samples = wave[0]
    tail_part = passed_along(samples[:HALO], "tm", -1)
    features = encode(jnp.concatenate([samples, tail_part]), w_first, w_mid, w_tail)
    own_labels = assign[0]
    shard_len = centroids.shape[0]
    feat_width = centroids.shape[1]
    first_id = lax.axis_index("tm") * shard_len
    centroid_ids = first_id + jnp.arange(shard_len, dtype=jnp.int32)
    rounded = lax.optimization_barrier(centroids.astype(jnp.bfloat16))
    widened = rounded.astype(jnp.float32)
    centroid_sq = jnp.sum(widened * widened, axis=1)
    frames = project(features, w_proj)
    accumulate_frames = lax.all_gather(frames, "tm", axis=0, tiled=True)
    labels = lax.all_gather(own_labels, "tm", axis=0, tiled=True)
    one_hot = labels[None, :] == centroid_ids[:, None]
    hot_rows = labels[:, None] == centroid_ids[None, :]
    hot_sums = jnp.dot(
        one_hot.astype(jnp.bfloat16), accumulate_frames, preferred_element_type=jnp.float32
    )
    counts = jnp.sum(one_hot.astype(jnp.float32), axis=1)
    products = jnp.einsum(
        "rd,kd->rk", accumulate_frames, rounded, preferred_element_type=jnp.float32
    )
    frame_wide = accumulate_frames.astype(jnp.float32)
    squares = jnp.sum(frame_wide * frame_wide, axis=1)
    is_owner = (labels >= first_id) & (labels < first_id + shard_len)
    picked = jnp.sum(jnp.where(hot_rows, centroid_sq[None, :] - 2.0 * products, 0.0), axis=1)
    own_term = jnp.where(is_owner, squares + picked, 0.0)
    term_sums = lax.psum_scatter(own_term, "tm", scatter_dimension=0, tiled=True)
    distortion = (term_sums / feat_width)[None, :]
    total_sums, total_counts = (
        lax.psum(hot_sums.astype(jnp.bfloat16), "grp").astype(jnp.float32),
        lax.psum(counts.astype(jnp.bfloat16), "grp").astype(jnp.float32),
    )
    new_counts = prior + total_counts
    new_centroids = (prior[:, None] * centroids + total_sums) / new_counts[:, None]
    return (new_centroids, new_counts, distortion)


def solution(mesh):
    return jax.shard_map(
        local,
        mesh=mesh,
        in_specs=(P("grp", "tm"), P("grp", "tm"), P(), P(), P(), P(), P("tm", None), P("tm")),
        out_specs=(P("tm", None), P("tm"), P("grp", "tm")),
        check_vma=False,
    )
```

profile of v0, /device:TPU:0, one launch (start us, length us, event | category | flops | bytes accessed | tf_op | source)
XLA Modules:
  0.0 410.5 jit_solution(17534476603627418723)
XLA Ops:
  7.2 0.7 slice_bitcast_fusion
  8.0 1.3 collective-permute-start
  9.2 1.4 reduce
  10.6 3.7 collective-permute-done
  14.3 0.1 slice_maximum_fusion
  14.4 4.5 %slice.152 = bf16[8207,5]{1,0:T(8,128)(2,1)S(1)} reshape(bf16[41035]{0:T(1024)(128)(2,1)S(1)} %get-tuple-element.8) | data formatting | bytes 164140 | tf_op jit(solution)/shard_map/slice | solution.py:30
  19.0 5.9 %slice.149 = bf16[8207,5]{1,0:T(8,128)(2,1)} reshape(bf16[41035]{0:T(1024)(128)(2,1)S(1)} %get-tuple-element.7) | data formatting | bytes 164140 | tf_op jit(solution)/shard_map/slice | solution.py:29
  24.8 8.0 %fusion.115 = f32[8207,512]{1,0:T(8,128)} fusion(bf16[8207,5]{1,0:T(8,128)(2,1)S(1)} %slice.152, bf16[10,512]{1,0:T(8,128)(2,1)S(1)} %copy-done.9), kind=kOutput, calls=%fused_computation.204 | convolution fusion | flops 42019840 | bytes 18917376 | tf_op jit(solution)/shard_map/dot_general | solution.py:30
  32.9 10.8 %fusion.121 = (f32[8207]{0:T(1024)S(1)}, f32[8207,512]{1,0:T(8,128)}) fusion(f32[8207,512]{1,0:T(8,128)} %fusion.115, bf16[8207,5]{1,0:T(8,128)(2,1)S(1)} %copy-done.5, bf16[10,512]{1,0:T(8,128)(2,1)S(1)} %copy-done.9), kind=kOutput, calls=%fused_computation.223 | convolution fusion | flops 50415600 | bytes 35758140 | tf_op jit(solution)/shard_map/dot_general | solution.py:29
  43.7 10.4 %multiply_reduce_fusion = f32[8207]{0:T(1024)S(1)} fusion(f32[8207,512]{1,0:T(8,128)} %get-tuple-element.10, f32[8207]{0:T(1024)S(1)} %broadcast_multiply_fusion), kind=kLoop, calls=%fused_computation.17 | loop fusion | flops 12597745 | bytes 16873592 | tf_op jit(solution)/shard_map/reduce_sum | solution.py:19
  54.1 0.3 copy-done.1
  54.4 45.7 %fusion.2 = bf16[8207,512]{1,0:T(8,128)(2,1)} fusion(f32[8207,512]{1,0:T(8,128)S(1)} %copy-done.1, f32[8207]{0:T(1024)S(1)} %add_rsqrt_fusion, f32[8207]{0:T(1024)S(1)} %broadcast_multiply_fusion), kind=kLoop, calls=%fused_computation.3 | loop fusion | flops 281532928 | bytes 25277560 | tf_op jit(solution)/shard_map/convert_element_type | solution.py:24
  100.1 13.0 %slice.155 = bf16[4103,1024]{1,0:T(8,128)(2,1)} reshape(bf16[8206,512]{1,0:T(8,128)(2,1)} %bitcast.63) | data formatting | bytes 16805888 | tf_op jit(solution)/shard_map/slice | solution.py:40
  113.1 8.0 %concatenate.16 = bf16[8208,512]{1,0:T(8,128)(2,1)} pad(bf16[8207,512]{1,0:T(8,128)(2,1)} %fusion.2, bf16[]{:T(256)} %constant.70.clone.1), padding=0_1x0_0 | pad | bytes 16808962 | tf_op jit(solution)/shard_map/concatenate | solution.py:37
  121.1 13.0 %reshape.165 = bf16[4104,1024]{1,0:T(8,128)(2,1)} reshape(bf16[8208,512]{1,0:T(8,128)(2,1)} %concatenate.16) | data formatting | bytes 16809984 | tf_op jit(solution)/shard_map/reshape | solution.py:37
  134.1 7.4 %fusion.64 = f32[4103,512]{1,0:T(8,128)S(1)} fusion(bf16[4103,1024]{1,0:T(8,128)(2,1)} %slice.155, bf16[4,1536,512]{2,1,0:T(8,128)(2,1)} %param.11), kind=kOutput, calls=%fused_computation.114 | convolution fusion | flops 4302307328 | bytes 17856512 | tf_op jit(solution)/shard_map/dot_general | solution.py:40
  141.6 3.7 fusion.122
  145.3 1.7 multiply_reduce_fusion.1
  147.0 22.3 %fusion.14 = bf16[4103,512]{1,0:T(8,128)(2,1)S(1)} fusion(f32[4103,512]{1,0:T(8,128)S(1)} %get-tuple-element.12, f32[4103]{0:T(1024)S(1)} %add_rsqrt_fusion.1, f32[4103]{0:T(1024)S(1)} %broadcast_multiply_fusion.1), kind=kLoop, calls=%fused_computation.27 | loop fusion | flops 140749312 | bytes 12637240 | tf_op jit(solution)/shard_map/convert_element_type | solution.py:24
  169.4 1.9 copy-done.2
  171.3 2.2 concatenate.17
  173.6 7.2 %slice.162 = bf16[2051,1024]{1,0:T(8,128)(2,1)} reshape(bf16[4102,512]{1,0:T(8,128)(2,1)} %bitcast.64) | data formatting | bytes 8400896 | tf_op jit(solution)/shard_map/slice | solution.py:40
  180.7 6.8 %fusion.62 = f32[2051,512]{1,0:T(8,128)} fusion(bf16[2051,1024]{1,0:T(8,128)(2,1)} %slice.162, bf16[4,1536,512]{2,1,0:T(8,128)(2,1)} %param.11), kind=kOutput, calls=%fused_computation.112 | convolution fusion | flops 2150629376 | bytes 9459712 | tf_op jit(solution)/shard_map/dot_general | solution.py:40
  187.5 7.2 %reshape.166 = bf16[2052,1024]{1,0:T(8,128)(2,1)} reshape(bf16[4104,512]{1,0:T(8,128)(2,1)} %concatenate.17) | data formatting | bytes 8404992 | tf_op jit(solution)/shard_map/reshape | solution.py:37
  194.7 4.5 %fusion.123 = (f32[2051]{0:T(1024)S(1)}, f32[2051,512]{1,0:T(8,128)S(1)}) fusion(f32[2051,512]{1,0:T(8,128)} %fusion.62, bf16[4,1536,512]{2,1,0:T(8,128)(2,1)} %param.11, bf16[2052,1024]{1,0:T(8,128)(2,1)} %reshape.166), kind=kOutput, calls=%fused_computation.225 | convolution fusion | flops 1077412864 | bytes 11048972 | tf_op jit(solution)/shard_map/dot_general | solution.py:41
  199.2 0.9 multiply_reduce_fusion.3
  200.1 11.7 %fusion.25 = bf16[2051,512]{1,0:T(8,128)(2,1)S(1)} fusion(f32[2051,512]{1,0:T(8,128)S(1)} %get-tuple-element.14, f32[2051]{0:T(1024)S(1)} %add_rsqrt_fusion.2, f32[2051]{0:T(1024)S(1)} %broadcast_multiply_fusion.2), kind=kLoop, calls=%fused_computation.53 | loop fusion | flops 70357504 | bytes 6317080 | tf_op jit(solution)/shard_map/convert_element_type | solution.py:24
  211.8 1.4 concatenate.18
  213.3 2.0 slice.169
  215.3 4.6 %fusion.60 = f32[1025,512]{1,0:T(8,128)} fusion(bf16[1025,1024]{1,0:T(8,128)(2,1)} %slice.169, bf16[4,1536,512]{2,1,0:T(8,128)(2,1)} %param.11), kind=kOutput, calls=%fused_computation.110 | convolution fusion | flops 1074790400 | bytes 5261312 | tf_op jit(solution)/shard_map/dot_general | solution.py:40
  219.9 2.0 reshape.167
  221.9 2.9 fusion.124
  224.8 0.5 multiply_reduce_fusion.5
  225.3 5.7 %fusion.41 = bf16[1025,512]{1,0:T(8,128)(2,1)S(1)} fusion(f32[1025,512]{1,0:T(8,128)S(1)} %get-tuple-element.16, f32[1025]{0:T(1024)S(1)} %add_rsqrt_fusion.3, f32[1025]{0:T(1024)S(1)} %broadcast_multiply_fusion.3), kind=kLoop, calls=%fused_computation.79 | loop fusion | flops 35161600 | bytes 3157000 | tf_op jit(solution)/shard_map/convert_element_type | solution.py:24
  231.2 1.2 slice.176
  232.3 3.3 fusion.58
  235.6 0.3 reshape.168
  236.0 1.9 fusion.125
  237.9 0.2 multiply_reduce_fusion.6
  238.0 2.6 fusion.53
  240.6 0.2 copy.13
  240.8 0.2 reshape.169
  241.0 1.7 fusion.126
  242.8 0.2 multiply_reduce_fusion.7
  243.0 1.3 fusion.81
  244.3 0.1 reshape.170
  244.4 1.6 fusion.127
  246.1 0.2 multiply_reduce_fusion.8
  246.3 0.8 convert_reduce_fusion
  247.0 0.2 fusion.100
  247.2 1.0 convolution_convert_fusion
  248.3 19.6 %all-gather = s32[1,1024]{1,0:T(1,128)S(1)} all-gather(s32[1,128]{1,0:T(1,128)S(1)} %copy-done.10), channel_id=2, replica_groups=mesh['grp'=4,'tm'=8] {'tm'}, dimensions={1}, use_global_device_ids=true | all-gather | bytes 4608 | tf_op jit(solution)/shard_map/all_gather | solution.py:81
  267.9 26.3 %all-gather.3.cloned.1.call-done = bf16[1024,768]{1,0:T(8,128)(2,1)} async-done(((bf16[128,768]{1,0:T(8,128)(2,1)}), bf16[1024,768]{1,0:T(8,128)(2,1)}) %all-gather.3.cloned.1.call-update) | async-done | bytes 1572880 | tf_op jit(solution)/shard_map/all_gather | solution.py:80
  294.2 6.3 %fusion.36 = bf16[2048,768]{1,0:T(8,128)(2,1)} fusion(bf16[1024,768]{1,0:T(8,128)(2,1)} %all-gather.3.cloned.1.call-done, s32[1024]{0:T(1024)S(1)} %bitcast.66, s32[2048]{0:T(1024)S(1)} %iota_add_fusion), kind=kOutput, calls=%fused_computation.74 | convolution fusion | flops 3224895488 | bytes 4730880 | tf_op jit(solution)/shard_map/dot_general | solution.py:84
  300.6 0.6 dynamic-slice
  301.9 1.1 fusion.22
  303.0 6.4 %psum.15 = bf16[2048]{0:T(1024)(128)(2,1)S(1)} all-reduce(bf16[2048]{0:T(1024)(128)(2,1)S(1)} %fusion.22), channel_id=1, replica_groups=mesh['grp'=4,'tm'=8] {'grp'}, use_global_device_ids=true, to_apply=%region_18.0 | all-reduce | flops 2048 | bytes 8192 | tf_op jit(solution)/shard_map/psum | solution.py:100
  309.4 0.4 multiply_reduce_fusion.4
  309.8 58.2 %all-reduce.7.cloned.1.call-done = bf16[2048,768]{1,0:T(8,128)(2,1)} async-done(((bf16[2048,768]{1,0:T(8,128)(2,1)}), bf16[2048,768]{1,0:T(8,128)(2,1)}) %all-reduce.7.cloned.1.call-update) | async-done | bytes 3145744 | tf_op jit(solution)/shard_map/psum | solution.py:99
  368.1 8.7 %fusion.120 = (bf16[2048,768]{1,0:T(8,128)(2,1)S(1)}, f32[2048,768]{1,0:T(8,128)}) fusion(f32[2048,768]{1,0:T(8,128)} %param.14, f32[2048]{0:T(1024)S(1)} %convert_add_fusion, bf16[2048,768]{1,0:T(8,128)(2,1)} %all-reduce.7.cloned.1.call-done, f32[2048]{0:T(1024)S(1)} %copy-done.7), kind=kLoop, calls=%fused_computation.222 | loop fusion | flops 7864320 | bytes 18890752 | tf_op jit(solution)/shard_map/convert_element_type | solution.py:76
  376.8 0.7 multiply_reduce_fusion.2
  377.4 4.0 select_reduce_fusion
  381.5 21.4 %all-reduce.4 = f32[1024]{0:T(1024)S(1)} all-reduce(f32[1024]{0:T(1024)S(1)} %add_select_fusion), channel_id=3, replica_groups=mesh['grp'=4,'tm'=8] {'tm'}, use_global_device_ids=true, to_apply=%region_22.23.clone | all-reduce | flops 1024 | bytes 8192
  402.9 0.6 fusion.118
  (47 shorter events, 0.4 us)
Async XLA Ops:
  7.2 240.1 %copy-start = (bf16[512,768]{1,0:T(8,128)(2,1)S(1)}, bf16[512,768]{1,0:T(8,128)(2,1)}, u32[]{:S(2)}) copy-start(bf16[512,768]{1,0:T(8,128)(2,1)} %param.13) | copy-start | bytes 2359300
  7.2 17.6 %copy-start.9 = (bf16[10,512]{1,0:T(8,128)(2,1)S(1)}, bf16[10,512]{1,0:T(8,128)(2,1)}, u32[]{:S(2)}) copy-start(bf16[10,512]{1,0:T(8,128)(2,1)} %param.10) | copy-start | bytes 30724
  7.2 287.0 %all-gather.3.cloned.1.call-start = ((), (), s32[]{:S(2)}) async-start(), calls=%async_computation | async-start | bytes 1769472 | tf_op jit(solution)/shard_map/all_gather | solution.py:80
  8.0 6.3 %collective-permute-start = (bf16[80]{0:T(256)(128)(2,1)S(1)}, bf16[80]{0:T(256)(128)(2,1)S(1)}, u32[]{:S(2)}, u32[]{:S(2)}) collective-permute-start(bf16[80]{0:T(256)(128)(2,1)S(1)} %slice_bitcast_fusion), channel_id=1, source_target_pairs={{1,0},{2,1},{3,2},{4,3},{5,4},{6,5},{7,6},{9,8},{10,9},{11,10},{12... | collective-permute-start | bytes 488 | tf_op jit(solution)/shard_map/ppermute | solution.py:13
  24.8 8.0 %copy-start.5 = (bf16[8207,5]{1,0:T(8,128)(2,1)S(1)}, bf16[8207,5]{1,0:T(8,128)(2,1)}, u32[]{:S(2)}) copy-start(bf16[8207,5]{1,0:T(8,128)(2,1)} %slice.149) | copy-start | bytes 246214
  43.7 10.7 %copy-start.1 = (f32[8207,512]{1,0:T(8,128)S(1)}, f32[8207,512]{1,0:T(8,128)}, u32[]{:S(2)}) copy-start(f32[8207,512]{1,0:T(8,128)} %get-tuple-element.10) | copy-start | bytes 50423812
  134.1 7.4 %copy-start.3 = (bf16[4104,1024]{1,0:T(8,128)(2,1)S(1)}, bf16[4104,1024]{1,0:T(8,128)(2,1)}, u32[]{:S(2)}) copy-start(bf16[4104,1024]{1,0:T(8,128)(2,1)} %reshape.165) | copy-start | bytes 25214980
  169.4 1.9 copy-start.2
  215.3 4.6 %copy-start.4 = (bf16[2052,512]{1,0:T(8,128)(2,1)S(1)}, bf16[2052,512]{1,0:T(8,128)(2,1)}, u32[]{:S(2)}) copy-start(bf16[2052,512]{1,0:T(8,128)(2,1)} %concatenate.18) | copy-start | bytes 6303748
  241.0 7.3 %copy-start.10 = (s32[1,128]{1,0:T(1,128)S(1)}, s32[1,128]{1,0:T(1,128)}, u32[]{:S(2)}) copy-start(s32[1,128]{1,0:T(1,128)} %param.9) | copy-start | bytes 1540
  248.3 119.8 %all-reduce.7.cloned.1.call-start = ((), (), s32[]{:S(2)}) async-start(), calls=%async_computation.1 | async-start | bytes 6291456 | tf_op jit(solution)/shard_map/psum | solution.py:99
  294.2 6.4 %copy-start.11 = (u32[32]{0:T(128)S(1)}, u32[32]{0:T(128)}, u32[]{:S(2)}) copy-start(u32[32]{0:T(128)} %constant.30) | copy-start | bytes 388
  294.2 15.2 %copy-start.7 = (f32[2048]{0:T(1024)S(1)}, f32[2048]{0:T(1024)}, u32[]{:S(2)}) copy-start(f32[2048]{0:T(1024)} %param.15) | copy-start | bytes 24580
  300.6 8.8 %copy-start.6 = (bf16[1024,768]{1,0:T(8,128)(2,1)S(1)}, bf16[1024,768]{1,0:T(8,128)(2,1)}, u32[]{:S(2)}) copy-start(bf16[1024,768]{1,0:T(8,128)(2,1)} %all-gather.3.cloned.1.call-done) | copy-start | bytes 4718596
  309.4 67.3 %copy-start.8 = (f32[2048]{0:T(1024)}, f32[2048]{0:T(1024)S(1)}, u32[]{:S(2)}) copy-start(f32[2048]{0:T(1024)S(1)} %convert_add_fusion) | copy-start | bytes 24580
Sparse Core Ops, SparseCore 0:
  248.4 45.8 all-gather.2
  300.7 67.2 all-reduce.6
where the time goes:
time: 418 us; the launch traced here: 410 us
  other arithmetic  117 us (28%)
  waiting for transfers between devices  88.3 us (21%)
  local copies, waits for them, and re-layouts  72.2 us (17%)
  matrix products  68.8 us (16%)
  blocking collectives  47.4 us (11%)
  between operations  15.2 us (4%)
    convert_element_type x6, other arithmetic, activate(): return jax.nn.gelu(norm_rows(accum), approximate=False).astype(jnp.bfloat16)  89.3 us
    psum x1, waiting for transfers between devices, local(): lax.psum(hot_sums.astype(jnp.bfloat16), 'grp').astype(jnp.float32)  58.2 us
    all_gather x1, waiting for transfers between devices, local(): accumulate_frames = lax.all_gather(frames, 'tm', axis=0, tiled=True)  26.3 us
    slice x5, local copies, waits for them, and re-layouts, odd_layer(): paired[:out_len]  23.4 us
    reshape x4, local copies, waits for them, and re-layouts, odd_layer(): jnp.concatenate([inputs, jnp.zeros((1, channels), inputs.dtype)], axis=0)  22.5 us
    dot_general x4, matrix products, odd_layer(): jnp.dot(paired[:out_len], weight[:2 * channels], preferred_element_type=j...  22.1 us
    unnamed x1, blocking collectives  21.4 us
    all_gather x1, blocking collectives, local(): labels = lax.all_gather(own_labels, 'tm', axis=0, tiled=True)  19.6 us
  transfers between devices with their start and end apart: 3, of which 3 were waited for; matrix products, arithmetic and copies ran while one was open for 1% of the time, Pallas kernels for 0%

commit v1 on v0

--- a/solution.py
+++ b/solution.py
@@ -96,7 +96,7 @@
     term_sums = lax.psum_scatter(own_term, "tm", scatter_dimension=0, tiled=True)
     distortion = (term_sums / feat_width)[None, :]
     total_sums, total_counts = (
-        lax.psum(hot_sums.astype(jnp.bfloat16), "grp").astype(jnp.float32),
+        jnp.sum(lax.all_gather(hot_sums.astype(jnp.bfloat16), "grp"), axis=0).astype(jnp.float32),
         lax.psum(counts.astype(jnp.bfloat16), "grp").astype(jnp.float32),
     )
     new_counts = prior + total_counts

time: 418 us -> 441 us (1.055)
  waiting for transfers between devices: 88.3 us -> 102 us
  other arithmetic: 117 us -> 127 us
    all_gather x0 -> x1, waiting for transfers between devices: none -> 72.3 us  [local(): lax.all_gather(hot_sums.astype(jnp.bfloat16), 'grp')]
    psum x1 -> x0, waiting for transfers between devices: 58.2 us -> none  [local(): lax.psum(hot_sums.astype(jnp.bfloat16), 'grp').astype(jnp.float32)]
    reduce_sum x0 -> x1, other arithmetic: none -> 8.97 us  [local(): jnp.sum(lax.all_gather(hot_sums.astype(jnp.bfloat16), 'grp'), axis=0)]
where the time goes in v1:
time: 441 us; the launch traced here: 433 us
  other arithmetic  127 us (29%)
  waiting for transfers between devices  102 us (23%)
  local copies, waits for them, and re-layouts  72.2 us (16%)
  matrix products  68.7 us (16%)
  blocking collectives  46.9 us (11%)
  between operations  15.3 us (3%)
    convert_element_type x6, other arithmetic, activate(): return jax.nn.gelu(norm_rows(accum), approximate=False).astype(jnp.bfloat16)  89.3 us
    all_gather x1, waiting for transfers between devices, local(): lax.all_gather(hot_sums.astype(jnp.bfloat16), 'grp')  72.3 us
    all_gather x1, waiting for transfers between devices, local(): accumulate_frames = lax.all_gather(frames, 'tm', axis=0, tiled=True)  26.3 us
    slice x5, local copies, waits for them, and re-layouts, odd_layer(): paired[:out_len]  23.4 us
    reshape x4, local copies, waits for them, and re-layouts, odd_layer(): jnp.concatenate([inputs, jnp.zeros((1, channels), inputs.dtype)], axis=0)  22.5 us
    dot_general x4, matrix products, odd_layer(): jnp.dot(paired[:out_len], weight[:2 * channels], preferred_element_type=j...  22.1 us
    unnamed x1, blocking collectives  21.4 us
    all_gather x1, blocking collectives, local(): labels = lax.all_gather(own_labels, 'tm', axis=0, tiled=True)  19.6 us
  transfers between devices with their start and end apart: 3, of which 3 were waited for; matrix products, arithmetic and copies ran while one was open for 1% of the time, Pallas kernels for 0%

profile of v1, /device:TPU:0, one launch (start us, length us, event | category | flops | bytes accessed | tf_op | source)
XLA Modules:
  0.0 433.4 jit_solution(18312388292109319015)
XLA Ops:
  7.2 0.7 slice_bitcast_fusion
  8.0 1.3 collective-permute-start
  9.2 1.4 reduce.1
  10.6 3.7 collective-permute-done
  14.3 0.1 slice_maximum_fusion
  14.4 4.5 %slice.152 = bf16[8207,5]{1,0:T(8,128)(2,1)S(1)} reshape(bf16[41035]{0:T(1024)(128)(2,1)S(1)} %get-tuple-element.8) | data formatting | bytes 164140 | tf_op jit(solution)/shard_map/slice | solution.py:30
  19.0 5.9 %slice.149 = bf16[8207,5]{1,0:T(8,128)(2,1)} reshape(bf16[41035]{0:T(1024)(128)(2,1)S(1)} %get-tuple-element.7) | data formatting | bytes 164140 | tf_op jit(solution)/shard_map/slice | solution.py:29
  24.8 8.0 %fusion.115 = f32[8207,512]{1,0:T(8,128)} fusion(bf16[8207,5]{1,0:T(8,128)(2,1)S(1)} %slice.152, bf16[10,512]{1,0:T(8,128)(2,1)S(1)} %copy-done.9), kind=kOutput, calls=%fused_computation.204 | convolution fusion | flops 42019840 | bytes 18917376 | tf_op jit(solution)/shard_map/dot_general | solution.py:30
  32.9 10.8 %fusion.121 = (f32[8207]{0:T(1024)S(1)}, f32[8207,512]{1,0:T(8,128)}) fusion(f32[8207,512]{1,0:T(8,128)} %fusion.115, bf16[8207,5]{1,0:T(8,128)(2,1)S(1)} %copy-done.5, bf16[10,512]{1,0:T(8,128)(2,1)S(1)} %copy-done.9), kind=kOutput, calls=%fused_computation.223 | convolution fusion | flops 50415600 | bytes 35758140 | tf_op jit(solution)/shard_map/dot_general | solution.py:29
  43.7 10.4 %multiply_reduce_fusion = f32[8207]{0:T(1024)S(1)} fusion(f32[8207,512]{1,0:T(8,128)} %get-tuple-element.10, f32[8207]{0:T(1024)S(1)} %broadcast_multiply_fusion), kind=kLoop, calls=%fused_computation.17 | loop fusion | flops 12597745 | bytes 16873592 | tf_op jit(solution)/shard_map/reduce_sum | solution.py:19
  54.1 0.3 copy-done.1
  54.4 45.7 %fusion.2 = bf16[8207,512]{1,0:T(8,128)(2,1)} fusion(f32[8207,512]{1,0:T(8,128)S(1)} %copy-done.1, f32[8207]{0:T(1024)S(1)} %add_rsqrt_fusion, f32[8207]{0:T(1024)S(1)} %broadcast_multiply_fusion), kind=kLoop, calls=%fused_computation.3 | loop fusion | flops 281532928 | bytes 25277560 | tf_op jit(solution)/shard_map/convert_element_type | solution.py:24
  100.0 13.0 %slice.155 = bf16[4103,1024]{1,0:T(8,128)(2,1)} reshape(bf16[8206,512]{1,0:T(8,128)(2,1)} %bitcast.64) | data formatting | bytes 16805888 | tf_op jit(solution)/shard_map/slice | solution.py:40
  113.1 8.0 %concatenate.16 = bf16[8208,512]{1,0:T(8,128)(2,1)} pad(bf16[8207,512]{1,0:T(8,128)(2,1)} %fusion.2, bf16[]{:T(256)} %constant.70.clone.1), padding=0_1x0_0 | pad | bytes 16808962 | tf_op jit(solution)/shard_map/concatenate | solution.py:37
  121.1 13.0 %reshape.165 = bf16[4104,1024]{1,0:T(8,128)(2,1)} reshape(bf16[8208,512]{1,0:T(8,128)(2,1)} %concatenate.16) | data formatting | bytes 16809984 | tf_op jit(solution)/shard_map/reshape | solution.py:37
  134.1 7.4 %fusion.64 = f32[4103,512]{1,0:T(8,128)S(1)} fusion(bf16[4103,1024]{1,0:T(8,128)(2,1)} %slice.155, bf16[4,1536,512]{2,1,0:T(8,128)(2,1)} %param.11), kind=kOutput, calls=%fused_computation.114 | convolution fusion | flops 4302307328 | bytes 17856512 | tf_op jit(solution)/shard_map/dot_general | solution.py:40
  141.5 3.8 fusion.122
  145.3 1.7 multiply_reduce_fusion.1
  147.0 22.3 %fusion.14 = bf16[4103,512]{1,0:T(8,128)(2,1)S(1)} fusion(f32[4103,512]{1,0:T(8,128)S(1)} %get-tuple-element.12, f32[4103]{0:T(1024)S(1)} %add_rsqrt_fusion.1, f32[4103]{0:T(1024)S(1)} %broadcast_multiply_fusion.1), kind=kLoop, calls=%fused_computation.27 | loop fusion | flops 140749312 | bytes 12637240 | tf_op jit(solution)/shard_map/convert_element_type | solution.py:24
  169.4 1.9 copy-done.2
  171.3 2.2 concatenate.17
  173.5 7.2 %slice.162 = bf16[2051,1024]{1,0:T(8,128)(2,1)} reshape(bf16[4102,512]{1,0:T(8,128)(2,1)} %bitcast.65) | data formatting | bytes 8400896 | tf_op jit(solution)/shard_map/slice | solution.py:40
  180.7 6.8 %fusion.62 = f32[2051,512]{1,0:T(8,128)} fusion(bf16[2051,1024]{1,0:T(8,128)(2,1)} %slice.162, bf16[4,1536,512]{2,1,0:T(8,128)(2,1)} %param.11), kind=kOutput, calls=%fused_computation.112 | convolution fusion | flops 2150629376 | bytes 9459712 | tf_op jit(solution)/shard_map/dot_general | solution.py:40
  187.5 7.2 %reshape.166 = bf16[2052,1024]{1,0:T(8,128)(2,1)} reshape(bf16[4104,512]{1,0:T(8,128)(2,1)} %concatenate.17) | data formatting | bytes 8404992 | tf_op jit(solution)/shard_map/reshape | solution.py:37
  194.6 4.5 %fusion.123 = (f32[2051]{0:T(1024)S(1)}, f32[2051,512]{1,0:T(8,128)S(1)}) fusion(f32[2051,512]{1,0:T(8,128)} %fusion.62, bf16[4,1536,512]{2,1,0:T(8,128)(2,1)} %param.11, bf16[2052,1024]{1,0:T(8,128)(2,1)} %reshape.166), kind=kOutput, calls=%fused_computation.225 | convolution fusion | flops 1077412864 | bytes 11048972 | tf_op jit(solution)/shard_map/dot_general | solution.py:41
  199.2 0.9 multiply_reduce_fusion.3
  200.1 11.7 %fusion.25 = bf16[2051,512]{1,0:T(8,128)(2,1)S(1)} fusion(f32[2051,512]{1,0:T(8,128)S(1)} %get-tuple-element.14, f32[2051]{0:T(1024)S(1)} %add_rsqrt_fusion.2, f32[2051]{0:T(1024)S(1)} %broadcast_multiply_fusion.2), kind=kLoop, calls=%fused_computation.53 | loop fusion | flops 70357504 | bytes 6317080 | tf_op jit(solution)/shard_map/convert_element_type | solution.py:24
  211.8 1.4 concatenate.18
  213.2 2.0 slice.169
  215.2 4.6 %fusion.60 = f32[1025,512]{1,0:T(8,128)} fusion(bf16[1025,1024]{1,0:T(8,128)(2,1)} %slice.169, bf16[4,1536,512]{2,1,0:T(8,128)(2,1)} %param.11), kind=kOutput, calls=%fused_computation.110 | convolution fusion | flops 1074790400 | bytes 5261312 | tf_op jit(solution)/shard_map/dot_general | solution.py:40
  219.9 2.0 reshape.167
  221.9 2.9 fusion.124
  224.8 0.5 multiply_reduce_fusion.5
  225.3 5.7 %fusion.41 = bf16[1025,512]{1,0:T(8,128)(2,1)S(1)} fusion(f32[1025,512]{1,0:T(8,128)S(1)} %get-tuple-element.16, f32[1025]{0:T(1024)S(1)} %add_rsqrt_fusion.3, f32[1025]{0:T(1024)S(1)} %broadcast_multiply_fusion.3), kind=kLoop, calls=%fused_computation.79 | loop fusion | flops 35161600 | bytes 3157000 | tf_op jit(solution)/shard_map/convert_element_type | solution.py:24
  231.1 1.2 slice.176
  232.3 3.3 fusion.58
  235.6 0.3 reshape.168
  235.9 1.9 fusion.125
  237.8 0.2 multiply_reduce_fusion.6
  238.0 2.6 fusion.53
  240.6 0.2 copy.13
  240.8 0.2 reshape.169
  241.0 1.7 fusion.126
  242.8 0.2 multiply_reduce_fusion.7
  243.0 1.3 fusion.81
  244.4 1.6 fusion.127
  246.0 0.2 multiply_reduce_fusion.8
  246.2 0.8 convert_reduce_fusion
  247.0 0.2 fusion.100
  247.2 1.0 convolution_convert_fusion
  248.3 19.6 %all-gather = s32[1,1024]{1,0:T(1,128)S(1)} all-gather(s32[1,128]{1,0:T(1,128)S(1)} %copy-done.10), channel_id=2, replica_groups=mesh['grp'=4,'tm'=8] {'tm'}, dimensions={1}, use_global_device_ids=true | all-gather | bytes 4608 | tf_op jit(solution)/shard_map/all_gather | solution.py:81
  267.9 26.3 %all-gather.5.cloned.1.call-done = bf16[1024,768]{1,0:T(8,128)(2,1)} async-done(((bf16[128,768]{1,0:T(8,128)(2,1)}), bf16[1024,768]{1,0:T(8,128)(2,1)}) %all-gather.5.cloned.1.call-update) | async-done | bytes 1572880 | tf_op jit(solution)/shard_map/all_gather | solution.py:80
  294.2 6.3 %fusion.36 = bf16[2048,768]{1,0:T(8,128)(2,1)} fusion(bf16[1024,768]{1,0:T(8,128)(2,1)} %all-gather.5.cloned.1.call-done, s32[1024]{0:T(1024)S(1)} %bitcast.68, s32[2048]{0:T(1024)S(1)} %iota_add_fusion), kind=kOutput, calls=%fused_computation.74 | convolution fusion | flops 3224895488 | bytes 4730880 | tf_op jit(solution)/shard_map/dot_general | solution.py:84
  300.6 0.6 dynamic-slice
  301.9 1.1 fusion.22
  303.0 6.0 %psum.7 = bf16[2048]{0:T(1024)(128)(2,1)S(1)} all-reduce(bf16[2048]{0:T(1024)(128)(2,1)S(1)} %fusion.22), channel_id=1, replica_groups=mesh['grp'=4,'tm'=8] {'grp'}, use_global_device_ids=true, to_apply=%region_18.0 | all-reduce | flops 2048 | bytes 8192 | tf_op jit(solution)/shard_map/psum | solution.py:100
  309.0 0.4 multiply_reduce_fusion.4
  309.3 72.3 %all-gather.7.cloned.1.call-done = bf16[8192,768]{1,0:T(8,128)(2,1)} async-done(((bf16[2048,768]{1,0:T(8,128)(2,1)}), bf16[8192,768]{1,0:T(8,128)(2,1)}) %all-gather.7.cloned.1.call-update) | async-done | bytes 12582928 | tf_op jit(solution)/shard_map/all_gather | solution.py:99
  381.7 9.0 %reduce_sum.208 = bf16[2048,768]{1,0:T(8,128)(2,1)} reduce(bf16[4,2048,768]{2,1,0:T(8,128)(2,1)} %bitcast.67, bf16[]{:T(256)} %constant.70.clone.1), dimensions={0}, to_apply=%region_16.0 | reduce | flops 4718592 | bytes 15728642 | tf_op jit(solution)/shard_map/reduce_sum | solution.py:99
  390.7 9.0 %fusion.120 = (bf16[2048,768]{1,0:T(8,128)(2,1)S(1)}, f32[2048,768]{1,0:T(8,128)}) fusion(f32[2048,768]{1,0:T(8,128)} %param.14, f32[2048]{0:T(1024)S(1)} %convert_add_fusion, bf16[2048,768]{1,0:T(8,128)(2,1)} %reduce_sum.208, f32[2048]{0:T(1024)S(1)} %copy-done.7), kind=kLoop, calls=%fused_computation.222 | loop fusion | flops 7864320 | bytes 18890752 | tf_op jit(solution)/shard_map/convert_element_type | solution.py:76
  399.6 0.7 multiply_reduce_fusion.2
  400.3 4.0 select_reduce_fusion
  404.4 21.4 %all-reduce.4 = f32[1024]{0:T(1024)S(1)} all-reduce(f32[1024]{0:T(1024)S(1)} %add_select_fusion), channel_id=4, replica_groups=mesh['grp'=4,'tm'=8] {'tm'}, use_global_device_ids=true, to_apply=%region_22.23.clone | all-reduce | flops 1024 | bytes 8192
  425.7 0.6 fusion.118
  (48 shorter events, 0.5 us)
Async XLA Ops:
  7.2 240.0 %copy-start = (bf16[512,768]{1,0:T(8,128)(2,1)S(1)}, bf16[512,768]{1,0:T(8,128)(2,1)}, u32[]{:S(2)}) copy-start(bf16[512,768]{1,0:T(8,128)(2,1)} %param.13) | copy-start | bytes 2359300
  7.2 17.6 %copy-start.9 = (bf16[10,512]{1,0:T(8,128)(2,1)S(1)}, bf16[10,512]{1,0:T(8,128)(2,1)}, u32[]{:S(2)}) copy-start(bf16[10,512]{1,0:T(8,128)(2,1)} %param.10) | copy-start | bytes 30724
  7.2 287.0 %all-gather.5.cloned.1.call-start = ((), (), s32[]{:S(2)}) async-start(), calls=%async_computation | async-start | bytes 1769472 | tf_op jit(solution)/shard_map/all_gather | solution.py:80
  8.0 6.3 %collective-permute-start = (bf16[80]{0:T(256)(128)(2,1)S(1)}, bf16[80]{0:T(256)(128)(2,1)S(1)}, u32[]{:S(2)}, u32[]{:S(2)}) collective-permute-start(bf16[80]{0:T(256)(128)(2,1)S(1)} %slice_bitcast_fusion), channel_id=1, source_target_pairs={{1,0},{2,1},{3,2},{4,3},{5,4},{6,5},{7,6},{9,8},{10,9},{11,10},{12... | collective-permute-start | bytes 488 | tf_op jit(solution)/shard_map/ppermute | solution.py:13
  24.8 8.0 %copy-start.5 = (bf16[8207,5]{1,0:T(8,128)(2,1)S(1)}, bf16[8207,5]{1,0:T(8,128)(2,1)}, u32[]{:S(2)}) copy-start(bf16[8207,5]{1,0:T(8,128)(2,1)} %slice.149) | copy-start | bytes 246214
  43.7 10.7 %copy-start.1 = (f32[8207,512]{1,0:T(8,128)S(1)}, f32[8207,512]{1,0:T(8,128)}, u32[]{:S(2)}) copy-start(f32[8207,512]{1,0:T(8,128)} %get-tuple-element.10) | copy-start | bytes 50423812
  134.1 7.4 %copy-start.3 = (bf16[4104,1024]{1,0:T(8,128)(2,1)S(1)}, bf16[4104,1024]{1,0:T(8,128)(2,1)}, u32[]{:S(2)}) copy-start(bf16[4104,1024]{1,0:T(8,128)(2,1)} %reshape.165) | copy-start | bytes 25214980
  169.3 1.9 copy-start.2
  215.2 4.6 %copy-start.4 = (bf16[2052,512]{1,0:T(8,128)(2,1)S(1)}, bf16[2052,512]{1,0:T(8,128)(2,1)}, u32[]{:S(2)}) copy-start(bf16[2052,512]{1,0:T(8,128)(2,1)} %concatenate.18) | copy-start | bytes 6303748
  241.0 7.3 %copy-start.10 = (s32[1,128]{1,0:T(1,128)S(1)}, s32[1,128]{1,0:T(1,128)}, u32[]{:S(2)}) copy-start(s32[1,128]{1,0:T(1,128)} %param.9) | copy-start | bytes 1540
  248.2 133.4 %all-gather.7.cloned.1.call-start = ((), (), s32[]{:S(2)}) async-start(), calls=%async_computation.1 | async-start | bytes 15728640 | tf_op jit(solution)/shard_map/all_gather | solution.py:99
  294.2 6.4 %copy-start.11 = (u32[32]{0:T(128)S(1)}, u32[32]{0:T(128)}, u32[]{:S(2)}) copy-start(u32[32]{0:T(128)} %constant.31) | copy-start | bytes 388
  294.2 14.7 %copy-start.7 = (f32[2048]{0:T(1024)S(1)}, f32[2048]{0:T(1024)}, u32[]{:S(2)}) copy-start(f32[2048]{0:T(1024)} %param.15) | copy-start | bytes 24580
  300.6 8.4 %copy-start.6 = (bf16[1024,768]{1,0:T(8,128)(2,1)S(1)}, bf16[1024,768]{1,0:T(8,128)(2,1)}, u32[]{:S(2)}) copy-start(bf16[1024,768]{1,0:T(8,128)(2,1)} %all-gather.5.cloned.1.call-done) | copy-start | bytes 4718596
  309.0 81.7 %copy-start.8 = (f32[2048]{0:T(1024)}, f32[2048]{0:T(1024)S(1)}, u32[]{:S(2)}) copy-start(f32[2048]{0:T(1024)S(1)} %convert_add_fusion) | copy-start | bytes 24580
Sparse Core Ops, SparseCore 0:
  248.4 45.8 all-gather.4
  300.7 80.9 all-gather.6
